TPU v7x, 32 devices: a whole 2x2x4 slice. The times are simulated.
32 devices in a mesh: grp: 1, col: 32 (over z, y, x, core), row: 1.
Axes of the slice: x: 2, y: 2, z: 4, core: 2. Of those that a mesh axis runs over, the one named last changes fastest.
Arguments:
- activations: bfloat16 [4096, 7168], P(('grp', 'col'), 'row'), may hold values from -6 to 6
- out_grads: bfloat16 [4096, 4096], P(('grp', 'col')), may hold values from -6 to 6
- in_basis: bfloat16 [7168, 7168], P('row', 'col'), may hold values from -0.0625 to 0.0625
- out_basis: bfloat16 [4096, 4096], P('col', 'row'), may hold values from -0.09375 to 0.09375
- eigen_values: float32 [4096, 7168], P('row', 'col'), may hold values from 0.1 to 10
- queries: bfloat16 [2, 4096, 7168], P(None, 'row', 'col'), may hold values from -0.00390625 to 0.00390625
- doc_ids: int32 [4096], P('grp'), may hold values from 0 to 63, never falling along the last dimension, each value on 1 to 128 neighbouring positions
Outputs:
- scores: float32 [64, 2], P('grp')
Inputs may be any that keep to these rules, and one draw needn't show every extreme that they name: doc_ids is non-decreasing along the tokens; each of the 64 documents has 1 to 128 tokens, and one has exactly 128.
All inputs are finite; a program needn't handle non-finite values.
Results may differ from a plain program's by a relative error of at most 0.0057.
Values may be sent and summed in bfloat16 or wider, within the bound.
No kernel may reach another device: no remote copies, remote signals or barrier semaphores. Data moves between devices by JAX's collectives and lax.ppermute only.
A program may use at most 192 MiB of HBM per device.

v0:
```python
import jax
import jax.numpy as jnp
from jax import lax
from jax.sharding import PartitionSpec as P

damping = 0.1


def local(activations, out_grads, in_basis, out_basis, eigen_values, queries, doc_ids):
    inverse_scale = 1.0 / (eigen_values + damping)
    weight_scaled = (queries.astype(jnp.float32) * inverse_scale[None]).astype(jnp.bfloat16)
    partial_in = jnp.dot(
        lax.all_gather(activations, "col", axis=0, tiled=True),
        in_basis,
        preferred_element_type=jnp.float32,
    )
    act_rot = lax.psum(partial_in, "row").astype(jnp.bfloat16)
    basis_cols = lax.all_gather(out_basis, "col", axis=0, tiled=True)
    grad_local = jnp.dot(out_grads, basis_cols, preferred_element_type=jnp.float32)
    grad_rot = lax.all_gather(grad_local.astype(jnp.bfloat16), "col", axis=0, tiled=True)
    mixed_terms = jnp.einsum(
        "ti,qij->tqj", grad_rot, weight_scaled, preferred_element_type=jnp.float32
    )
    token_part = jnp.sum(mixed_terms * act_rot.astype(jnp.float32)[:, None, :], axis=2)
    doc_count = max(2, doc_ids.shape[0] // 64)
    membership = (doc_ids[:, None] == jnp.arange(doc_count, dtype=jnp.int32)[None, :]).astype(
        jnp.float32
    )
    doc_sizes = jnp.sum(membership, axis=0)
    doc_part = jnp.dot(
        membership.T,
        token_part,
        precision=lax.Precision.HIGHEST,
        preferred_element_type=jnp.float32,
    )
    summed = lax.psum(doc_part, ("col", "row"))
    return summed / doc_sizes[:, None]


def solution(mesh):
    placed = (
        P(("grp", "col"), "row"),
        P(("grp", "col"), None),
        P("row", "col"),
        P("col", "row"),
        P("row", "col"),
        P(None, "row", "col"),
        P("grp"),
    )
    return jax.shard_map(
        local, mesh=mesh, in_specs=placed, out_specs=P("grp", None), check_vma=False
    )
```

profile of v0, /device:TPU:0, one launch (start us, length us, event | category | flops | bytes accessed | tf_op | source)
XLA Modules:
  0.0 793.8 jit_solution(6344292427624281930)
XLA Ops:
  6.5 0.0 copy-start
  6.5 0.0 all-gather.4.cloned.1.call-start
  6.5 0.7 all-gather.4.cloned.1.call-update
  7.3 0.0 all-gather.8.cloned.1.call-start
  7.3 0.7 all-gather.8.cloned.1.call-update
  8.0 0.0 copy-start.3
  8.0 0.0 all-gather.6.cloned.1.call-start
  8.1 199.0 %all-gather.4.cloned.1.call-done = bf16[4096,4096]{1,0:T(8,128)(2,1)} async-done(((bf16[128,4096]{1,0:T(8,128)(2,1)}), bf16[4096,4096]{1,0:T(8,128)(2,1)}) %all-gather.4.cloned.1.call-update) | async-done | bytes 33554448 | tf_op jit(solution)/shard_map/all_gather | solution.py:18
  207.1 17.6 %convolution_convert_fusion.1 = bf16[128,4096]{1,0:T(8,128)(2,1)} fusion(bf16[128,4096]{1,0:T(8,128)(2,1)} %param.8, bf16[4096,4096]{1,0:T(8,128)(2,1)} %all-gather.4.cloned.1.call-done), kind=kOutput, calls=%fused_computation.4 | convolution fusion | flops 4295491584 | bytes 35651584 | tf_op jit(solution)/shard_map/dot_general | solution.py:19
  224.7 0.0 all-gather.6.cloned.1.call-update
  224.7 0.0 copy-done.3
  224.7 0.2 convert_reduce_fusion
  225.0 0.0 copy-start.2
  225.0 2.7 add_divide_fusion
  227.7 0.5 copy-done.2
  228.1 3.0 multiply_convert_fusion
  231.1 292.1 %all-gather.8.cloned.1.call-done = bf16[4096,7168]{1,0:T(8,128)(2,1)} async-done(((bf16[128,7168]{1,0:T(8,128)(2,1)}), bf16[4096,7168]{1,0:T(8,128)(2,1)}) %all-gather.8.cloned.1.call-update) | async-done | bytes 58720272 | tf_op jit(solution)/shard_map/all_gather | solution.py:13
  523.3 0.0 copy-done
  523.3 26.1 %fusion = f32[4096,224]{0,1:T(8,128)} fusion(bf16[4096,7168]{1,0:T(8,128)(2,1)} %all-gather.8.cloned.1.call-done, bf16[7168,224]{0,1:T(8,128)(2,1)S(1)} %copy-done), kind=kOutput, calls=%fused_computation.3 | convolution fusion | flops 13155172352 | bytes 65601536 | tf_op jit(solution)/shard_map/dot_general | solution.py:12
  549.3 169.2 %all-gather.6.cloned.1.call-done = bf16[4096,4096]{1,0:T(8,128)(2,1)} async-done(((bf16[128,4096]{1,0:T(8,128)(2,1)}), bf16[4096,4096]{1,0:T(8,128)(2,1)}) %all-gather.6.cloned.1.call-update) | async-done | bytes 33554448 | tf_op jit(solution)/shard_map/all_gather | solution.py:20
  718.5 24.2 %fusion.3 = f32[4096,448]{0,1} fusion(bf16[4096,4096]{1,0:T(8,128)(2,1)} %all-gather.6.cloned.1.call-done, bf16[4096,448]{0,1:T(8,128)(2,1)} %bitcast.12), kind=kOutput, calls=%fused_computation.11 | convolution fusion | flops 15032385536 | bytes 44564480
  742.7 0.0 copy-start.1
  742.7 5.1 multiply_reduce_fusion
  747.8 0.6 fusion.1
  748.4 38.3 %psum.6 = f32[64,2]{0,1:T(2,128)S(1)} all-reduce(f32[64,2]{0,1:T(2,128)S(1)} %fusion.1), channel_id=1, replica_groups=mesh['grp'=1,'col'=32,'row'=1] {'col','row'}, use_global_device_ids=true, to_apply=%region_1.0 | all-reduce | flops 128 | bytes 1024 | tf_op jit(solution)/shard_map/psum | solution.py:36
  786.7 0.6 broadcast_divide_fusion
  787.3 0.0 copy-done.1
Async XLA Ops:
  6.5 516.7 %copy-start = (bf16[7168,224]{0,1:T(8,128)(2,1)S(1)}, bf16[7168,224]{0,1:T(8,128)(2,1)}, u32[]{:S(2)}) copy-start(bf16[7168,224]{0,1:T(8,128)(2,1)} %param.9) | copy-start | bytes 9633796
  6.5 200.6 %all-gather.4.cloned.1.call-start = ((), (), s32[]{:S(2)}) async-start(), calls=%async_computation | async-start | bytes 34603008 | tf_op jit(solution)/shard_map/all_gather | solution.py:18
  7.3 516.0 %all-gather.8.cloned.1.call-start = ((), (), s32[]{:S(2)}) async-start(), calls=%async_computation.2 | async-start | bytes 60555264 | tf_op jit(solution)/shard_map/all_gather | solution.py:13
  8.0 216.7 %copy-start.3 = (s32[4096]{0:T(1024)S(1)}, s32[4096]{0:T(1024)}, u32[]{:S(2)}) copy-start(s32[4096]{0:T(1024)} %param.13) | copy-start | bytes 49156
  8.0 710.5 %all-gather.6.cloned.1.call-start = ((), (), s32[]{:S(2)}) async-start(), calls=%async_computation.1 | async-start | bytes 34603008 | tf_op jit(solution)/shard_map/all_gather | solution.py:20
  225.0 3.2 copy-start.2
  742.7 44.6 %copy-start.1 = (bf16[7168,224]{0,1:T(8,128)(2,1)S(1)}, bf16[7168,224]{0,1:T(8,128)(2,1)}, u32[]{:S(2)}) copy-start(bf16[7168,224]{0,1:T(8,128)(2,1)} %param.9) | copy-start | bytes 9633796
Sparse Core Ops, SparseCore 0:
  10.2 196.8 all-gather.3
  210.0 313.2 all-gather.7
  526.1 192.3 all-gather.5
where the time goes:
time: 794 us
  waiting for transfers between devices  662 us (83%)
  matrix products  68.4 us (9%)
  blocking collectives  38.3 us (5%)
  between operations  13.1 us (2%)
  other arithmetic  11.6 us (1%)
    all_gather x1, waiting for transfers between devices, local(): lax.all_gather(activations, 'col', axis=0, tiled=True)  292 us
    all_gather x1, waiting for transfers between devices, local(): basis_cols = lax.all_gather(out_basis, 'col', axis=0, tiled=True)  199 us
    all_gather x1, waiting for transfers between devices, local(): lax.all_gather(grad_local.astype(jnp.bfloat16), 'col', axis=0, tiled=True)  169 us
    psum x1, blocking collectives, local(): summed = lax.psum(doc_part, ('col', 'row'))  38.3 us
    dot_general x1, matrix products, local(): jnp.dot(lax.all_gather(activations, 'col', axis=0, tiled=True), in_basis,...  26.1 us
    unnamed x1, matrix products  24.2 us
    dot_general x1, matrix products, local(): jnp.dot(out_grads, basis_cols, preferred_element_type=jnp.float32)  17.6 us
  transfers between devices with their start and end apart: 3, of which 3 were waited for; matrix products, arithmetic and copies ran while one was open for 6% of the time, Pallas kernels for 0%

commit v1 on v0

v1 whole, which is shorter than its diff:
```python
import jax
import jax.numpy as jnp
from jax import lax
from jax.sharding import PartitionSpec as P

damping = 0.1


def roles(n):
    bits = n.bit_length() - 1
    if bits >= 4:
        tokens = [0, bits - 2]
    else:
        tokens = [0] if bits else []
    columns = [b for b in range(bits) if b not in tokens]
    return tokens, columns


def swap(value, bit, n):
    return lax.ppermute(value, "col", [(d, d ^ (1 << bit)) for d in range(n)])


def dotf(a, b, dims):
    return lax.dot_general(a, b, (dims, ((), ())), preferred_element_type=jnp.float32)


def spread(value, columns, n):
    pieces = {0: value}
    top = len(columns) - 1
    order = sorted(range(1, 1 << len(columns)), key=lambda e: (bin(e).count("1"), e))
    for e in order:
        has = [i for i in range(top + 1) if e >> i & 1]
        if e >> top & 1:
            last = has[0]
        else:
            last = has[-1]
        pieces[e] = swap(pieces[e ^ (1 << last)], columns[last], n)
    return [pieces[e] for e in range(1 << len(columns))]


def make_local(n):
    tokens, columns = roles(n)
    groups = 1 << len(columns)

    def offset(e):
        return sum((1 << columns[i]) for i in range(len(columns)) if e >> i & 1)

    def local(activations, out_grads, in_basis, out_basis, eigen_values, queries, doc_ids):
        me = lax.axis_index("col")
        part = sum(((me >> b) & 1) << i for i, b in enumerate(columns))
        rows = out_basis.shape[0]
        wide = out_basis.shape[1] // groups
        mine = activations.shape[0]

        grads = spread(out_grads, columns, n)
        block = out_basis
        for b in reversed(columns):
            bit = ((me >> b) & 1) == 0
            half = block.shape[1] // 2
            low, high = block[:, :half], block[:, half:]
            keep = jnp.where(bit, low, high)
            came = swap(jnp.where(bit, high, low), b, n)
            block = jnp.concatenate([jnp.where(bit, keep, came), jnp.where(bit, came, keep)], axis=0)
        majors = list(reversed(columns))
        for b in reversed(tokens):
            bit = ((me >> b) & 1) == 0
            came = swap(block, b, n)
            block = jnp.concatenate([jnp.where(bit, block, came), jnp.where(bit, came, block)], axis=0)
            majors.append(b)
        majors = majors[::-1]
        block = block.reshape((2,) * len(majors) + (rows, wide))
        where = [majors.index(b) for b in sorted(majors, reverse=True)]
        block = block.transpose(where + [len(majors), len(majors) + 1]).reshape(n * rows, wide)
        rotated = dotf(jnp.concatenate(grads, axis=0), block, ((1,), (0,))).astype(jnp.bfloat16)
        pieces = spread(rotated, columns, n)
        pieces = [
            jnp.concatenate([p[(r ^ e) * mine : (r ^ e) * mine + mine] for r in range(groups)], axis=0)
            for e, p in enumerate(pieces)
        ]
        grad_rot = jnp.concatenate(pieces, axis=1)

        values, grads_q = eigen_values.T, queries.transpose(0, 2, 1)
        scaled = []
        for e in range(groups):
            start = (part ^ e) * wide
            inverse = 1.0 / (lax.dynamic_slice_in_dim(values, start, wide, 1) + damping)
            piece = lax.dynamic_slice_in_dim(grads_q, start, wide, 2).astype(jnp.float32)
            scaled.append((piece * inverse[None]).astype(jnp.bfloat16))
        scaled = jnp.concatenate(scaled, axis=2)

        bases, weights = [in_basis.T], [scaled]
        for b in reversed(tokens):
            bases = bases + [swap(v, b, n) for v in bases]
            weights = weights + [swap(v, b, n) for v in weights]
        basis = jnp.concatenate(bases, axis=0)
        queries_n, span = queries.shape[0], basis.shape[0]
        weight = jnp.concatenate([w[q] for q in range(queries_n) for w in weights], axis=0)

        acts = spread(activations, columns, n)
        full, top = groups - 1, groups >> 1
        order = sorted(range(groups), key=lambda e: (bin(e).count("1"), e))
        pairs = [order[i : i + 2] for i in range(0, groups, 2)]
        token_part, ids = [], []
        for pair in pairs:
            act = jnp.concatenate([acts[e] for e in pair], axis=0)
            act_rot = lax.psum(dotf(act, basis, ((1,), (1,))), "row")
            act_rot = act_rot.astype(jnp.bfloat16).astype(jnp.float32)
            rot = jnp.concatenate([grad_rot[e * mine : e * mine + mine] for e in pair], axis=0)
            mixed = dotf(rot, weight, ((1,), (1,)))
            token_part.append(
                jnp.stack(
                    [jnp.sum(mixed[:, q * span : (q + 1) * span] * act_rot, axis=1) for q in range(queries_n)], axis=1
                )
            )
            ids += [lax.dynamic_slice_in_dim(doc_ids, (me ^ offset(e)) * mine, mine) for e in pair]
        token_part = jnp.concatenate(token_part, axis=0)
        ids = jnp.concatenate(ids)

        docs = jnp.arange(max(2, doc_ids.shape[0] // 64), dtype=jnp.int32)
        doc_sizes = jnp.sum((doc_ids[:, None] == docs[None, :]).astype(jnp.float32), axis=0)
        membership = (ids[:, None] == docs[None, :]).astype(jnp.float32)
        summed = jnp.dot(
            membership.T, token_part, precision=lax.Precision.HIGHEST, preferred_element_type=jnp.float32
        )
        for b in range(len(tokens) + len(columns)):
            summed = summed + swap(summed, b, n)
        return lax.psum(summed, "row") / doc_sizes[:, None]

    return local


def solution(mesh):
    placed = (
        P(("grp", "col"), "row"),
        P(("grp", "col"), None),
        P("row", "col"),
        P("col", "row"),
        P("row", "col"),
        P(None, "row", "col"),
        P("grp"),
    )
    return jax.shard_map(
        make_local(mesh.shape["col"]), mesh=mesh, in_specs=placed, out_specs=P("grp", None), check_vma=False
    )
```

time: 794 us -> 520 us (0.65)
  waiting for transfers between devices: 662 us -> 317 us
  local copies, waits for them, and re-layouts: 0.5 us -> 60.1 us
  starting transfers between devices: 0.08 us -> 38.8 us
  blocking collectives: 38.3 us -> 0 us
  matrix products: 68.4 us -> 82.1 us
  between operations: 13.1 us -> 0.3 us
  other arithmetic: 11.6 us -> 21.9 us
    all_gather x3 -> x0, waiting for transfers between devices: 660 us -> none  [the longest x1 292 us: local(): lax.all_gather(activations, 'col', axis=0, tiled=True)]
    ppermute x0 -> x37, waiting for transfers between devices: none -> 317 us  [swap(): return lax.ppermute(value, 'col', [(d, d ^ 1 << bit) for d in range(n)])]
    unnamed x8 -> x72, local copies, waits for them, and re-layouts: 0.5 us -> 53.1 us
    ppermute x0 -> x37, starting transfers between devices: none -> 38.8 us  [swap(): return lax.ppermute(value, 'col', [(d, d ^ 1 << bit) for d in range(n)])]
    psum x1 -> x0, blocking collectives: 38.3 us -> none  [local(): summed = lax.psum(doc_part, ('col', 'row'))]
    dot_general x2 -> x9, matrix products: 43.7 us -> 81.7 us  [dotf(): lax.dot_general(a, b, (dims, ((), ())), preferred_element_type=jnp.float32)]
    unnamed x1 -> x0, matrix products: 24.2 us -> none
    unnamed x0 -> x11, other arithmetic: none -> 11 us
  transfers between devices with their start and end apart: 3 -> 37, of which waited for: 3 -> 21; matrix products, arithmetic and copies ran while one was open for 6% -> 30% of each run, Pallas kernels for 0% -> 0%
where the time goes in v1:
time: 520 us
  waiting for transfers between devices  317 us (61%)
  matrix products  82.1 us (16%)
  local copies, waits for them, and re-layouts  60.1 us (12%)
  starting transfers between devices  38.8 us (7%)
  other arithmetic  21.9 us (4%)
    ppermute x37, waiting for transfers between devices, swap(): return lax.ppermute(value, 'col', [(d, d ^ 1 << bit) for d in range(n)])  317 us
    dot_general x9, matrix products, dotf(): lax.dot_general(a, b, (dims, ((), ())), preferred_element_type=jnp.float32)  81.7 us
    unnamed x72, local copies, waits for them, and re-layouts  53.1 us
    ppermute x37, starting transfers between devices, swap(): return lax.ppermute(value, 'col', [(d, d ^ 1 << bit) for d in range(n)])  38.8 us
    unnamed x11, other arithmetic  11 us
  transfers between devices with their start and end apart: 37, of which 21 were waited for; matrix products, arithmetic and copies ran while one was open for 30% of the time, Pallas kernels for 0%

profile of v1, /device:TPU:0, one launch (start us, length us, event | category | flops | bytes accessed | tf_op | source)
XLA Modules:
  0.0 519.7 jit_solution(806118114438387453)
XLA Ops:
  0.0 3.0 collective-permute-start
  21.2 2.9 fusion.35
  24.9 94.3 %collective-permute-done.7 = bf16[128,2048]{1,0:T(8,128)(2,1)} collective-permute-done((bf16[128,2048]{1,0:T(8,128)(2,1)}, bf16[128,2048]{1,0:T(8,128)(2,1)}, u32[]{:S(2)}, u32[]{:S(2)}) %collective-permute-start.7) | collective-permute-done | bytes 524320 | tf_op jit(solution)/shard_map/ppermute | solution.py:20
  124.9 7.9 %collective-permute-done.8 = bf16[256,1024]{1,0:T(8,128)(2,1)S(1)} collective-permute-done((bf16[256,1024]{1,0:T(8,128)(2,1)S(1)}, bf16[256,1024]{1,0:T(8,128)(2,1)S(1)}, u32[]{:S(2)}, u32[]{:S(2)}) %collective-permute-start.8) | collective-permute-done | bytes 524320 | tf_op jit(solution)/shard_map/ppermute | solution.py:20
  137.0 9.0 %collective-permute-done.9 = bf16[512,512]{1,0:T(8,128)(2,1)} collective-permute-done((bf16[512,512]{1,0:T(8,128)(2,1)}, bf16[512,512]{1,0:T(8,128)(2,1)}, u32[]{:S(2)}, u32[]{:S(2)}) %collective-permute-start.9) | collective-permute-done | bytes 524320 | tf_op jit(solution)/shard_map/ppermute | solution.py:20
  155.7 6.0 %collective-permute-done.5 = bf16[128,4096]{1,0:T(8,128)(2,1)S(1)} collective-permute-done((bf16[128,4096]{1,0:T(8,128)(2,1)S(1)}, bf16[128,4096]{1,0:T(8,128)(2,1)S(1)}, u32[]{:S(2)}, u32[]{:S(2)}) %collective-permute-start.5) | collective-permute-done | bytes 1048608 | tf_op jit(solution)/shard_map/ppermute | solution.py:20
  164.0 5.9 %collective-permute-done.10 = bf16[1024,512]{1,0:T(8,128)(2,1)S(1)} collective-permute-done((bf16[1024,512]{1,0:T(8,128)(2,1)S(1)}, bf16[1024,512]{1,0:T(8,128)(2,1)S(1)}, u32[]{:S(2)}, u32[]{:S(2)}) %collective-permute-start.10) | collective-permute-done | bytes 1048608 | tf_op jit(solution)/shard_map/ppermute | solution.py:20
  170.9 10.5 %collective-permute-done.2 = bf16[128,4096]{1,0:T(8,128)(2,1)S(1)} collective-permute-done((bf16[128,4096]{1,0:T(8,128)(2,1)}, bf16[128,4096]{1,0:T(8,128)(2,1)S(1)}, u32[]{:S(2)}, u32[]{:S(2)}) %collective-permute-start.2) | collective-permute-done | bytes 1048608 | tf_op jit(solution)/shard_map/ppermute | solution.py:20
  183.5 4.5 collective-permute-done.4
  188.0 3.0 collective-permute-start.23
  193.1 10.4 %collective-permute-done.6 = bf16[128,4096]{1,0:T(8,128)(2,1)S(1)} collective-permute-done((bf16[128,4096]{1,0:T(8,128)(2,1)S(1)}, bf16[128,4096]{1,0:T(8,128)(2,1)S(1)}, u32[]{:S(2)}, u32[]{:S(2)}) %collective-permute-start.6) | collective-permute-done | bytes 1048608 | tf_op jit(solution)/shard_map/ppermute | solution.py:20
  205.9 8.3 %constant_dynamic-update-slice_fusion.9 = (bf16[1024,4096]{0,1:T(8,128)(2,1)}, bf16[1024,512]{0,1:T(8,128)(2,1)S(1)}) fusion(bf16[1024,4096]{1,0:T(8,128)(2,1)} %constant_dynamic-update-slice_fusion.1, bf16[4096,512]{1,0:T(8,128)(2,1)S(1)} %bitcast.116), kind=kOutput, calls=%fused_computation.178 | convolution fusion | flops 4295491584 | bytes 14680064 | tf_op jit(solution)/shard_map/dot_general | solution.py:24
  215.2 2.9 fusion.34
  223.2 16.5 %collective-permute-done.12 = bf16[1024,512]{0,1:T(8,128)(2,1)S(1)} collective-permute-done((bf16[1024,512]{0,1:T(8,128)(2,1)S(1)}, bf16[1024,512]{0,1:T(8,128)(2,1)S(1)}, u32[]{:S(2)}, u32[]{:S(2)}) %collective-permute-start.12) | collective-permute-done | bytes 1048608 | tf_op jit(solution)/shard_map/ppermute | solution.py:20
  249.9 33.7 %collective-permute-done.15 = bf16[1024,512]{0,1:T(8,128)(2,1)S(1)} collective-permute-done((bf16[1024,512]{0,1:T(8,128)(2,1)S(1)}, bf16[1024,512]{0,1:T(8,128)(2,1)S(1)}, u32[]{:S(2)}, u32[]{:S(2)}) %collective-permute-start.15) | collective-permute-done | bytes 1048608 | tf_op jit(solution)/shard_map/ppermute | solution.py:20
  292.0 17.3 %collective-permute-done.16 = bf16[1024,512]{0,1:T(8,128)(2,1)S(1)} collective-permute-done((bf16[1024,512]{0,1:T(8,128)(2,1)S(1)}, bf16[1024,512]{0,1:T(8,128)(2,1)S(1)}, u32[]{:S(2)}, u32[]{:S(2)}) %collective-permute-start.16) | collective-permute-done | bytes 1048608 | tf_op jit(solution)/shard_map/ppermute | solution.py:20
  315.4 35.8 %collective-permute-done.27 = bf16[128,7168]{1,0:T(8,128)(2,1)} collective-permute-done((bf16[128,7168]{1,0:T(8,128)(2,1)S(1)}, bf16[128,7168]{1,0:T(8,128)(2,1)}, u32[]{:S(2)}, u32[]{:S(2)}) %collective-permute-start.27) | collective-permute-done | bytes 1835040 | tf_op jit(solution)/shard_map/ppermute | solution.py:20
  356.3 3.0 fusion.31
  359.4 2.9 fusion.30
  366.5 28.4 %collective-permute-done.30 = bf16[128,7168]{1,0:T(8,128)(2,1)} collective-permute-done((bf16[128,7168]{1,0:T(8,128)(2,1)}, bf16[128,7168]{1,0:T(8,128)(2,1)}, u32[]{:S(2)}, u32[]{:S(2)}) %collective-permute-start.30) | collective-permute-done | bytes 1835040 | tf_op jit(solution)/shard_map/ppermute | solution.py:20
  394.9 19.3 %collective-permute-done.18 = bf16[1024,512]{0,1:T(8,128)(2,1)S(1)} collective-permute-done((bf16[1024,512]{0,1:T(8,128)(2,1)S(1)}, bf16[1024,512]{0,1:T(8,128)(2,1)S(1)}, u32[]{:S(2)}, u32[]{:S(2)}) %collective-permute-start.18) | collective-permute-done | bytes 1048608 | tf_op jit(solution)/shard_map/ppermute | solution.py:20
  420.4 11.1 %fusion.16 = f32[256,1792]{1,0:T(8,128)} fusion(bf16[1792,4096]{1,0:T(8,128)(2,1)} %fusion.28, bf16[1024,4096]{0,1:T(8,128)(2,1)} %slice_dynamic-update-slice_fusion), kind=kOutput, calls=%fused_computation.18 | convolution fusion | flops 3758096384 | bytes 18612224 | tf_op jit(solution)/shard_map/dot_general | solution.py:24
  431.5 11.3 %fusion.18 = f32[256,1792]{1,0:T(8,128)} fusion(bf16[1792,4096]{1,0:T(8,128)(2,1)} %fusion.28, bf16[1024,4096]{0,1:T(8,128)(2,1)} %slice_dynamic-update-slice_fusion), kind=kOutput, calls=%fused_computation.20 | convolution fusion | flops 3758096384 | bytes 18612224 | tf_op jit(solution)/shard_map/dot_general | solution.py:24
  447.7 8.2 %fusion.67 = (f32[256]{0:T(256)S(1)}, f32[256]{0:T(256)S(1)}) fusion(f32[256,1792]{1,0:T(8,128)S(1)} %copy-done.9, bf16[224,7168]{1,0:T(8,128)(2,1)} %collective-permute-done.25, bf16[224,7168]{1,0:T(8,128)(2,1)} %collective-permute-done.24, bf16[224,7168]{1,0:T(8,128)(2,1)} %collective-permute-done.23, bf16[224,7168]{1,0:T(8,128)(2,1)} %bitcast.27, ...), kind=kOutput, calls=%fused_computation.85 | convolution fusion | flops 3348430336 | bytes 18352128 | tf_op jit(solution)/shard_map/dot_general | solution.py:24
  457.4 8.6 %fusion.61 = (f32[256]{0:T(256)S(1)}, f32[256]{0:T(256)S(1)}) fusion(f32[256,1792]{1,0:T(8,128)S(1)} %copy-done.7, bf16[224,7168]{1,0:T(8,128)(2,1)} %collective-permute-done.25, bf16[224,7168]{1,0:T(8,128)(2,1)} %collective-permute-done.24, bf16[224,7168]{1,0:T(8,128)(2,1)} %collective-permute-done.23, bf16[224,7168]{1,0:T(8,128)(2,1)} %bitcast.27, ...), kind=kOutput, calls=%fused_computation.73 | convolution fusion | flops 3348430336 | bytes 18352128 | tf_op jit(solution)/shard_map/dot_general | solution.py:24
  466.0 8.8 %fusion.24 = f32[256,1792]{1,0:T(8,128)} fusion(bf16[1792,4096]{1,0:T(8,128)(2,1)} %fusion.28, bf16[128,4096]{0,1:T(8,128)(2,1)S(1)} %get-tuple-element.14, bf16[128,4096]{0,1:T(8,128)(2,1)S(1)} %get-tuple-element.15), kind=kOutput, calls=%fused_computation.27 | convolution fusion | flops 3762290688 | bytes 18612224 | tf_op jit(solution)/shard_map/dot_general | solution.py:24
  474.7 8.1 %fusion.20 = f32[256,1792]{1,0:T(8,128)S(1)} fusion(bf16[1792,4096]{1,0:T(8,128)(2,1)} %fusion.28, bf16[128,4096]{0,1:T(8,128)(2,1)S(1)} %get-tuple-element.16, bf16[128,4096]{0,1:T(8,128)(2,1)S(1)} %get-tuple-element.13), kind=kOutput, calls=%fused_computation.23 | convolution fusion | flops 3762290688 | bytes 18612224 | tf_op jit(solution)/shard_map/dot_general | solution.py:24
  482.9 8.7 %fusion.65 = (f32[256]{0:T(256)S(1)}, f32[256]{0:T(256)S(1)}) fusion(f32[256,1792]{1,0:T(8,128)S(1)} %fusion.20, bf16[224,7168]{1,0:T(8,128)(2,1)} %collective-permute-done.25, bf16[224,7168]{1,0:T(8,128)(2,1)} %collective-permute-done.24, bf16[224,7168]{1,0:T(8,128)(2,1)} %collective-permute-done.23, bf16[224,7168]{1,0:T(8,128)(2,1)} %bitcast.27, ...), kind=kOutput, calls=%fused_computation.81 | convolution fusion | flops 3348430336 | bytes 18352128 | tf_op jit(solution)/shard_map/dot_general | solution.py:24
  493.7 8.6 %fusion.63 = (f32[256]{0:T(256)S(1)}, f32[256]{0:T(256)S(1)}) fusion(f32[256,1792]{1,0:T(8,128)S(1)} %copy-done.8, bf16[224,7168]{1,0:T(8,128)(2,1)} %collective-permute-done.25, bf16[224,7168]{1,0:T(8,128)(2,1)} %collective-permute-done.24, bf16[224,7168]{1,0:T(8,128)(2,1)} %collective-permute-done.23, bf16[224,7168]{1,0:T(8,128)(2,1)} %bitcast.27, ...), kind=kOutput, calls=%fused_computation.77 | convolution fusion | flops 3348430336 | bytes 18352128 | tf_op jit(solution)/shard_map/dot_general | solution.py:24
  504.5 3.0 collective-permute-done.33
  511.1 3.6 collective-permute-done.35
  515.7 3.4 collective-permute-done.36
  (163 shorter events, 110.9 us)
Async XLA Ops:
  0.0 150.5 %collective-permute-start = (bf16[128,4096]{1,0:T(8,128)(2,1)}, bf16[128,4096]{1,0:T(8,128)(2,1)}, u32[]{:S(2)}, u32[]{:S(2)}) collective-permute-start(bf16[128,4096]{1,0:T(8,128)(2,1)} %param.8), channel_id=1, source_target_pairs={{0,2},{1,3},{2,0},{3,1},{4,6},{5,7},{6,4},{7,5},{8,10},{9,11},{10,... | collective-permute-start | bytes 3145736 | tf_op jit(solution)/shard_map/ppermute | solution.py:20
  3.0 149.9 %collective-permute-start.1 = (bf16[128,4096]{1,0:T(8,128)(2,1)}, bf16[128,4096]{1,0:T(8,128)(2,1)}, u32[]{:S(2)}, u32[]{:S(2)}) collective-permute-start(bf16[128,4096]{1,0:T(8,128)(2,1)} %param.8), channel_id=1, source_target_pairs={{0,4},{1,5},{2,6},{3,7},{4,0},{5,1},{6,2},{7,3},{8,12},{9,13},{10,... | collective-permute-start | bytes 3145736 | tf_op jit(solution)/shard_map/ppermute | solution.py:20
  4.5 132.0 %collective-permute-start.3 = (bf16[128,4096]{1,0:T(8,128)(2,1)}, bf16[128,4096]{1,0:T(8,128)(2,1)S(1)}, u32[]{:S(2)}, u32[]{:S(2)}) collective-permute-start(bf16[128,4096]{1,0:T(8,128)(2,1)} %param.8), channel_id=1, source_target_pairs={{0,16},{1,17},{2,18},{3,19},{4,20},{5,21},{6,22},{7,23},{8,24},{9,... | collective-permute-start | bytes 3145736 | tf_op jit(solution)/shard_map/ppermute | solution.py:20
  18.4 196.8 %collective-permute-start.19 = (bf16[2,224,4096]{2,1,0:T(8,128)(2,1)}, bf16[2,224,4096]{2,1,0:T(8,128)(2,1)}, u32[]{:S(2)}, u32[]{:S(2)}) collective-permute-start(bf16[2,224,4096]{2,1,0:T(8,128)(2,1)} %fusion.86), channel_id=1, source_target_pairs={{0,8},{1,9},{2,10},{3,11},{4,12},{5,13},{6,14},{7,15},{8,0},{9,1},... | collective-permute-start | bytes 11010056 | tf_op jit(solution)/shard_map/ppermute | solution.py:20
  20.9 98.3 %collective-permute-start.7 = (bf16[128,2048]{1,0:T(8,128)(2,1)}, bf16[128,2048]{1,0:T(8,128)(2,1)}, u32[]{:S(2)}, u32[]{:S(2)}) collective-permute-start(bf16[128,2048]{1,0:T(8,128)(2,1)} %broadcast_select_fusion.6), channel_id=1, source_target_pairs={{0,16},{1,17},{2,18},{3,19},{4,20},{5,21},{6,22},{7,23},{8,24},{9,... | collective-permute-start | bytes 1572872 | tf_op jit(solution)/shard_map/ppermute | solution.py:20
  120.5 12.3 %collective-permute-start.8 = (bf16[256,1024]{1,0:T(8,128)(2,1)S(1)}, bf16[256,1024]{1,0:T(8,128)(2,1)S(1)}, u32[]{:S(2)}, u32[]{:S(2)}) collective-permute-start(bf16[256,1024]{1,0:T(8,128)(2,1)S(1)} %broadcast_select_fusion.10), channel_id=1, source_target_pairs={{0,4},{1,5},{2,6},{3,7},{4,0},{5,1},{6,2},{7,3},{8,12},{9,13},{10,... | collective-permute-start | bytes 1572872 | tf_op jit(solution)/shard_map/ppermute | solution.py:20
  134.1 11.8 %collective-permute-start.9 = (bf16[512,512]{1,0:T(8,128)(2,1)}, bf16[512,512]{1,0:T(8,128)(2,1)}, u32[]{:S(2)}, u32[]{:S(2)}) collective-permute-start(bf16[512,512]{1,0:T(8,128)(2,1)} %broadcast_select_fusion.14), channel_id=1, source_target_pairs={{0,2},{1,3},{2,0},{3,1},{4,6},{5,7},{6,4},{7,5},{8,10},{9,11},{10,... | collective-permute-start | bytes 1572872 | tf_op jit(solution)/shard_map/ppermute | solution.py:20
  136.5 25.2 %collective-permute-start.5 = (bf16[128,4096]{1,0:T(8,128)(2,1)S(1)}, bf16[128,4096]{1,0:T(8,128)(2,1)S(1)}, u32[]{:S(2)}, u32[]{:S(2)}) collective-permute-start(bf16[128,4096]{1,0:T(8,128)(2,1)S(1)} %collective-permute-done.3), channel_id=1, source_target_pairs={{0,4},{1,5},{2,6},{3,7},{4,0},{5,1},{6,2},{7,3},{8,12},{9,13},{10,... | collective-permute-start | bytes 3145736 | tf_op jit(solution)/shard_map/ppermute | solution.py:20
  147.3 22.5 %collective-permute-start.10 = (bf16[1024,512]{1,0:T(8,128)(2,1)S(1)}, bf16[1024,512]{1,0:T(8,128)(2,1)S(1)}, u32[]{:S(2)}, u32[]{:S(2)}) collective-permute-start(bf16[1024,512]{1,0:T(8,128)(2,1)S(1)} %pad_maximum_fusion.3), channel_id=1, source_target_pairs={{0,8},{1,9},{2,10},{3,11},{4,12},{5,13},{6,14},{7,15},{8,0},{9,1},... | collective-permute-start | bytes 3145736 | tf_op jit(solution)/shard_map/ppermute | solution.py:20
  150.5 67.6 %collective-permute-start.20 = (bf16[2,224,4096]{2,1,0:T(8,128)(2,1)}, bf16[2,224,4096]{2,1,0:T(8,128)(2,1)S(1)}, u32[]{:S(2)}, u32[]{:S(2)}) collective-permute-start(bf16[2,224,4096]{2,1,0:T(8,128)(2,1)} %fusion.86), channel_id=1, source_target_pairs={{0,1},{1,0},{2,3},{3,2},{4,5},{5,4},{6,7},{7,6},{8,9},{9,8},{10,11... | collective-permute-start | bytes 11010056 | tf_op jit(solution)/shard_map/ppermute | solution.py:20
  152.9 28.5 %collective-permute-start.2 = (bf16[128,4096]{1,0:T(8,128)(2,1)}, bf16[128,4096]{1,0:T(8,128)(2,1)S(1)}, u32[]{:S(2)}, u32[]{:S(2)}) collective-permute-start(bf16[128,4096]{1,0:T(8,128)(2,1)} %collective-permute-done), channel_id=1, source_target_pairs={{0,4},{1,5},{2,6},{3,7},{4,0},{5,1},{6,2},{7,3},{8,12},{9,13},{10,... | collective-permute-start | bytes 3145736 | tf_op jit(solution)/shard_map/ppermute | solution.py:20
  161.7 26.3 %collective-permute-start.4 = (bf16[128,4096]{1,0:T(8,128)(2,1)S(1)}, bf16[128,4096]{1,0:T(8,128)(2,1)S(1)}, u32[]{:S(2)}, u32[]{:S(2)}) collective-permute-start(bf16[128,4096]{1,0:T(8,128)(2,1)S(1)} %collective-permute-done.3), channel_id=1, source_target_pairs={{0,2},{1,3},{2,0},{3,1},{4,6},{5,7},{6,4},{7,5},{8,10},{9,11},{10,... | collective-permute-start | bytes 3145736 | tf_op jit(solution)/shard_map/ppermute | solution.py:20
  169.8 33.6 %collective-permute-start.6 = (bf16[128,4096]{1,0:T(8,128)(2,1)S(1)}, bf16[128,4096]{1,0:T(8,128)(2,1)S(1)}, u32[]{:S(2)}, u32[]{:S(2)}) collective-permute-start(bf16[128,4096]{1,0:T(8,128)(2,1)S(1)} %collective-permute-done.5), channel_id=1, source_target_pairs={{0,2},{1,3},{2,0},{3,1},{4,6},{5,7},{6,4},{7,5},{8,10},{9,11},{10,... | collective-permute-start | bytes 3145736 | tf_op jit(solution)/shard_map/ppermute | solution.py:20
  181.4 23.1 %collective-permute-start.11 = (bf16[2048,512]{1,0:T(8,128)(2,1)S(1)}, bf16[2048,512]{1,0:T(8,128)(2,1)S(1)}, u32[]{:S(2)}, u32[]{:S(2)}) collective-permute-start(bf16[2048,512]{1,0:T(8,128)(2,1)S(1)} %pad_maximum_fusion.2), channel_id=1, source_target_pairs={{0,1},{1,0},{2,3},{3,2},{4,5},{5,4},{6,7},{7,6},{8,9},{9,8},{10,11... | collective-permute-start | bytes 6291464 | tf_op jit(solution)/shard_map/ppermute | solution.py:20
  188.0 177.1 %collective-permute-start.23 = (bf16[224,7168]{1,0:T(8,128)(2,1)}, bf16[224,7168]{1,0:T(8,128)(2,1)}, u32[]{:S(2)}, u32[]{:S(2)}) collective-permute-start(bf16[224,7168]{1,0:T(8,128)(2,1)} %bitcast.27), channel_id=1, source_target_pairs={{0,8},{1,9},{2,10},{3,11},{4,12},{5,13},{6,14},{7,15},{8,0},{9,1},... | collective-permute-start | bytes 9633800 | tf_op jit(solution)/shard_map/ppermute | solution.py:20
  203.5 243.6 %collective-permute-start.24 = (bf16[224,7168]{1,0:T(8,128)(2,1)}, bf16[224,7168]{1,0:T(8,128)(2,1)}, u32[]{:S(2)}, u32[]{:S(2)}) collective-permute-start(bf16[224,7168]{1,0:T(8,128)(2,1)} %bitcast.27), channel_id=1, source_target_pairs={{0,1},{1,0},{2,3},{3,2},{4,5},{5,4},{6,7},{7,6},{8,9},{9,8},{10,11... | collective-permute-start | bytes 9633800 | tf_op jit(solution)/shard_map/ppermute | solution.py:20
  214.2 25.6 %collective-permute-start.12 = (bf16[1024,512]{0,1:T(8,128)(2,1)S(1)}, bf16[1024,512]{0,1:T(8,128)(2,1)S(1)}, u32[]{:S(2)}, u32[]{:S(2)}) collective-permute-start(bf16[1024,512]{0,1:T(8,128)(2,1)S(1)} %get-tuple-element.46), channel_id=1, source_target_pairs={{0,2},{1,3},{2,0},{3,1},{4,6},{5,7},{6,4},{7,5},{8,10},{9,11},{10,... | collective-permute-start | bytes 3145736 | tf_op jit(solution)/shard_map/ppermute | solution.py:20
  219.6 27.4 %collective-permute-start.13 = (bf16[1024,512]{0,1:T(8,128)(2,1)S(1)}, bf16[1024,512]{0,1:T(8,128)(2,1)S(1)}, u32[]{:S(2)}, u32[]{:S(2)}) collective-permute-start(bf16[1024,512]{0,1:T(8,128)(2,1)S(1)} %get-tuple-element.46), channel_id=1, source_target_pairs={{0,4},{1,5},{2,6},{3,7},{4,0},{5,1},{6,2},{7,3},{8,12},{9,13},{10,... | collective-permute-start | bytes 3145736 | tf_op jit(solution)/shard_map/ppermute | solution.py:20
  220.6 63.0 %collective-permute-start.15 = (bf16[1024,512]{0,1:T(8,128)(2,1)S(1)}, bf16[1024,512]{0,1:T(8,128)(2,1)S(1)}, u32[]{:S(2)}, u32[]{:S(2)}) collective-permute-start(bf16[1024,512]{0,1:T(8,128)(2,1)S(1)} %get-tuple-element.46), channel_id=1, source_target_pairs={{0,16},{1,17},{2,18},{3,19},{4,20},{5,21},{6,22},{7,23},{8,24},{9,... | collective-permute-start | bytes 3145736 | tf_op jit(solution)/shard_map/ppermute | solution.py:20
  239.8 43.9 %collective-permute-start.14 = (bf16[1024,512]{0,1:T(8,128)(2,1)S(1)}, bf16[1024,512]{0,1:T(8,128)(2,1)S(1)}, u32[]{:S(2)}, u32[]{:S(2)}) collective-permute-start(bf16[1024,512]{0,1:T(8,128)(2,1)S(1)} %collective-permute-done.12), channel_id=1, source_target_pairs={{0,4},{1,5},{2,6},{3,7},{4,0},{5,1},{6,2},{7,3},{8,12},{9,13},{10,... | collective-permute-start | bytes 3145736 | tf_op jit(solution)/shard_map/ppermute | solution.py:20
  246.9 104.2 %collective-permute-start.27 = (bf16[128,7168]{1,0:T(8,128)(2,1)S(1)}, bf16[128,7168]{1,0:T(8,128)(2,1)}, u32[]{:S(2)}, u32[]{:S(2)}) collective-permute-start(bf16[128,7168]{1,0:T(8,128)(2,1)S(1)} %copy-done.4), channel_id=1, source_target_pairs={{0,16},{1,17},{2,18},{3,19},{4,20},{5,21},{6,22},{7,23},{8,24},{9,... | collective-permute-start | bytes 5505032 | tf_op jit(solution)/shard_map/ppermute | solution.py:20
  283.6 70.8 %collective-permute-start.21 = (bf16[2,224,4096]{2,1,0:T(8,128)(2,1)}, bf16[2,224,4096]{2,1,0:T(8,128)(2,1)S(1)}, u32[]{:S(2)}, u32[]{:S(2)}) collective-permute-start(bf16[2,224,4096]{2,1,0:T(8,128)(2,1)} %collective-permute-done.19), channel_id=1, source_target_pairs={{0,1},{1,0},{2,3},{3,2},{4,5},{5,4},{6,7},{7,6},{8,9},{9,8},{10,11... | collective-permute-start | bytes 11010056 | tf_op jit(solution)/shard_map/ppermute | solution.py:20
  283.7 25.6 %collective-permute-start.16 = (bf16[1024,512]{0,1:T(8,128)(2,1)S(1)}, bf16[1024,512]{0,1:T(8,128)(2,1)S(1)}, u32[]{:S(2)}, u32[]{:S(2)}) collective-permute-start(bf16[1024,512]{0,1:T(8,128)(2,1)S(1)} %collective-permute-done.15), channel_id=1, source_target_pairs={{0,2},{1,3},{2,0},{3,1},{4,6},{5,7},{6,4},{7,5},{8,10},{9,11},{10,... | collective-permute-start | bytes 3145736 | tf_op jit(solution)/shard_map/ppermute | solution.py:20
  309.3 42.4 %collective-permute-start.17 = (bf16[1024,512]{0,1:T(8,128)(2,1)S(1)}, bf16[1024,512]{0,1:T(8,128)(2,1)S(1)}, u32[]{:S(2)}, u32[]{:S(2)}) collective-permute-start(bf16[1024,512]{0,1:T(8,128)(2,1)S(1)} %collective-permute-done.15), channel_id=1, source_target_pairs={{0,4},{1,5},{2,6},{3,7},{4,0},{5,1},{6,2},{7,3},{8,12},{9,13},{10,... | collective-permute-start | bytes 3145736 | tf_op jit(solution)/shard_map/ppermute | solution.py:20
  351.2 94.3 %collective-permute-start.22 = (bf16[128,7168]{1,0:T(8,128)(2,1)S(1)}, bf16[128,7168]{1,0:T(8,128)(2,1)}, u32[]{:S(2)}, u32[]{:S(2)}) collective-permute-start(bf16[128,7168]{1,0:T(8,128)(2,1)S(1)} %copy-done.4), channel_id=1, source_target_pairs={{0,2},{1,3},{2,0},{3,1},{4,6},{5,7},{6,4},{7,5},{8,10},{9,11},{10,... | collective-permute-start | bytes 5505032 | tf_op jit(solution)/shard_map/ppermute | solution.py:20
  351.7 43.2 %collective-permute-start.30 = (bf16[128,7168]{1,0:T(8,128)(2,1)}, bf16[128,7168]{1,0:T(8,128)(2,1)}, u32[]{:S(2)}, u32[]{:S(2)}) collective-permute-start(bf16[128,7168]{1,0:T(8,128)(2,1)} %collective-permute-done.27), channel_id=1, source_target_pairs={{0,4},{1,5},{2,6},{3,7},{4,0},{5,1},{6,2},{7,3},{8,12},{9,13},{10,... | collective-permute-start | bytes 5505032 | tf_op jit(solution)/shard_map/ppermute | solution.py:20
  354.4 59.8 %collective-permute-start.18 = (bf16[1024,512]{0,1:T(8,128)(2,1)S(1)}, bf16[1024,512]{0,1:T(8,128)(2,1)S(1)}, u32[]{:S(2)}, u32[]{:S(2)}) collective-permute-start(bf16[1024,512]{0,1:T(8,128)(2,1)S(1)} %collective-permute-done.17), channel_id=1, source_target_pairs={{0,2},{1,3},{2,0},{3,1},{4,6},{5,7},{6,4},{7,5},{8,10},{9,11},{10,... | collective-permute-start | bytes 3145736 | tf_op jit(solution)/shard_map/ppermute | solution.py:20
  365.1 117.8 %collective-permute-start.26 = (bf16[128,7168]{1,0:T(8,128)(2,1)S(1)}, bf16[128,7168]{1,0:T(8,128)(2,1)}, u32[]{:S(2)}, u32[]{:S(2)}) collective-permute-start(bf16[128,7168]{1,0:T(8,128)(2,1)S(1)} %copy-done.4), channel_id=1, source_target_pairs={{0,4},{1,5},{2,6},{3,7},{4,0},{5,1},{6,2},{7,3},{8,12},{9,13},{10,... | collective-permute-start | bytes 5505032 | tf_op jit(solution)/shard_map/ppermute | solution.py:20
  394.9 52.8 %collective-permute-start.25 = (bf16[224,7168]{1,0:T(8,128)(2,1)}, bf16[224,7168]{1,0:T(8,128)(2,1)}, u32[]{:S(2)}, u32[]{:S(2)}) collective-permute-start(bf16[224,7168]{1,0:T(8,128)(2,1)} %collective-permute-done.23), channel_id=1, source_target_pairs={{0,1},{1,0},{2,3},{3,2},{4,5},{5,4},{6,7},{7,6},{8,9},{9,8},{10,11... | collective-permute-start | bytes 9633800 | tf_op jit(solution)/shard_map/ppermute | solution.py:20
  414.2 43.2 %collective-permute-start.31 = (bf16[128,7168]{1,0:T(8,128)(2,1)}, bf16[128,7168]{1,0:T(8,128)(2,1)}, u32[]{:S(2)}, u32[]{:S(2)}) collective-permute-start(bf16[128,7168]{1,0:T(8,128)(2,1)} %collective-permute-done.30), channel_id=1, source_target_pairs={{0,2},{1,3},{2,0},{3,1},{4,6},{5,7},{6,4},{7,5},{8,10},{9,11},{10,... | collective-permute-start | bytes 5505032 | tf_op jit(solution)/shard_map/ppermute | solution.py:20
  445.5 48.2 %collective-permute-start.29 = (bf16[128,7168]{1,0:T(8,128)(2,1)}, bf16[128,7168]{1,0:T(8,128)(2,1)}, u32[]{:S(2)}, u32[]{:S(2)}) collective-permute-start(bf16[128,7168]{1,0:T(8,128)(2,1)} %collective-permute-done.27), channel_id=1, source_target_pairs={{0,2},{1,3},{2,0},{3,1},{4,6},{5,7},{6,4},{7,5},{8,10},{9,11},{10,... | collective-permute-start | bytes 5505032 | tf_op jit(solution)/shard_map/ppermute | solution.py:20
  447.0 46.6 %collective-permute-start.28 = (bf16[128,7168]{1,0:T(8,128)(2,1)}, bf16[128,7168]{1,0:T(8,128)(2,1)}, u32[]{:S(2)}, u32[]{:S(2)}) collective-permute-start(bf16[128,7168]{1,0:T(8,128)(2,1)} %collective-permute-done.22), channel_id=1, source_target_pairs={{0,4},{1,5},{2,6},{3,7},{4,0},{5,1},{6,2},{7,3},{8,12},{9,13},{10,... | collective-permute-start | bytes 5505032 | tf_op jit(solution)/shard_map/ppermute | solution.py:20
  (15 other events, 280.2 us)
